TPU v7x, 512 devices: a whole 4x8x8 slice. The times are simulated.
512 devices in a mesh: layer: 32 (over z_lo, x, core), dp: 8 (over y), mp: 2 (over z_hi).
Axes of the slice: x: 4, y: 8, z: 8 (z_hi: 2, z_lo: 4; z = z_hi * 4 + z_lo), core: 2. Of those that a mesh axis runs over, the one named last changes fastest.
Arguments:
- states: bfloat16 [128, 1024, 1024], P('layer', 'dp'), may hold values from -6 to 6
- weights: bfloat16 [128, 1024, 1024], P('layer', 'dp', 'mp'), may hold values from -0.1875 to 0.1875
- guess_points: bfloat16 [32, 1024, 1024], P('layer', 'dp'), may hold values from -2 to 2
- cotangent: bfloat16 [1024, 1024], P('dp'), may hold values from -6 to 6
Outputs:
- adjoint: bfloat16 [128, 1024, 1024], P('layer', 'dp', 'mp')
- weight_grads: float32 [128, 1024, 1024], P('layer', 'dp', 'mp')
All inputs are finite; a program needn't handle non-finite values.
Results may differ from a plain program's by a relative error of at most 0.03.
Values may be sent and summed in bfloat16 or wider, within the bound.
No kernel may reach another device: no remote copies, remote signals or barrier semaphores. Data moves between devices by JAX's collectives and lax.ppermute only.
A program may use at most 64 MiB of HBM per device.

v0:
```python
import jax
import jax.numpy as jnp
from jax import lax
from jax.sharding import PartitionSpec as P

step_size = 0.1


def from_behind(value, axis, steps):
    count = lax.axis_size(axis)
    leading, last = (max(0, -steps), min(count, count - steps))
    return lax.ppermute(value, axis, [(source, source + steps) for source in range(leading, last)])


def shortened(array):
    return jax.tree.map(lambda a: a.astype(jnp.bfloat16) if a.dtype == jnp.float32 else a, array)


def slope_of(inputs, weight_block):
    tangent = jnp.tanh(jnp.dot(inputs, weight_block, preferred_element_type=jnp.float32))
    return 1.0 - tangent * tangent


def back_product(scaled_rows, weight_block):
    return lax.dot_general(
        scaled_rows, weight_block, (((1,), (1,)), ((), ())), preferred_element_type=jnp.float32
    )


def body(states, weights, guess_points, cotangent):
    slab_count = lax.axis_size("layer")
    slab_index = lax.axis_index("layer")
    half_index = lax.axis_index("mp")
    layer_count, row_count, model_width = states.shape
    point_count = guess_points.shape[0]
    factor = layer_count // point_count
    columns = weights.shape[2]
    half_rows = row_count // lax.axis_size("mp")
    row_start = half_index * half_rows
    col_start = half_index * columns
    gathered = lax.all_gather(weights, "dp", axis=1, tiled=True)
    next_point = from_behind(guess_points[0], "layer", -1)
    terminal = jnp.where(
        slab_index == slab_count - 1, cotangent.astype(jnp.float32), next_point.astype(jnp.float32)
    )
    guess_wide = guess_points.astype(jnp.float32)
    slopes = [slope_of(states[layer_id], gathered[layer_id]) for layer_id in range(layer_count)]

    def scale_columns(upper_adj, layer_id):
        own_part = lax.dynamic_slice_in_dim(upper_adj, col_start, columns, 1)
        return (own_part * slopes[layer_id]).astype(jnp.bfloat16)

    def fine_step(upper_adj, scaled_rows, layer_id):
        summed = lax.psum(back_product(scaled_rows, gathered[layer_id]), "mp")
        return upper_adj + step_size * summed

    upper_adj = terminal
    residuals = [None] * point_count
    for layer_id in range(layer_count - 1, -1, -1):
        relaxed = fine_step(upper_adj, scale_columns(upper_adj, layer_id), layer_id)
        if layer_id % factor == 0:
            residuals[layer_id // factor] = relaxed - guess_wide[layer_id // factor]
            upper_adj = guess_wide[layer_id // factor]
        else:
            upper_adj = relaxed
    residual_half = lax.dynamic_slice_in_dim(jnp.stack(residuals), row_start, half_rows, 1)
    coarse_weights = lax.all_gather(gathered[::factor], "mp", axis=2, tiled=True)
    state_half = lax.dynamic_slice_in_dim(states[::factor], row_start, half_rows, 1)
    coarse_slopes = jnp.stack([slope_of(state_half[0], coarse_weights[0])])

    def coarse_solve(incoming):
        carried = incoming.astype(jnp.float32)
        results = [None] * point_count
        scaled_rows = (carried * coarse_slopes[0]).astype(jnp.bfloat16)
        stepped = (
            carried
            + factor * step_size * back_product(scaled_rows, coarse_weights[0])
            + residual_half[0]
        )
        results[0] = stepped.astype(jnp.bfloat16)
        return jnp.stack(results)

    def solve_pair(operand_pair):
        return coarse_solve(operand_pair[0])

    def keep_pair(operand_pair):
        return operand_pair[1]

    def one_turn(turn_id, loop_state):
        incoming, errors = loop_state
        errors = lax.cond(
            turn_id == slab_count - 1 - slab_index, solve_pair, keep_pair, (incoming, errors)
        )
        incoming = from_behind(shortened(errors[0]), "layer", -1)
        return (incoming, errors)

    start_in = jnp.zeros((half_rows, model_width), jnp.bfloat16)
    start_errors = jnp.zeros((point_count, half_rows, model_width), jnp.bfloat16)
    incoming, errors = lax.fori_loop(0, slab_count - 1, one_turn, (start_in, start_errors))
    errors = lax.cond(slab_index == 0, solve_pair, keep_pair, (incoming, errors))
    adjoint_parts = [None] * layer_count
    scaled_parts = [None] * layer_count
    spread = lax.all_gather(
        shortened(jnp.concatenate([errors, incoming[None]], 0)), "mp", axis=1, tiled=True
    )
    upper_adj = terminal + spread[point_count].astype(jnp.float32)
    for layer_id in range(layer_count - 1, -1, -1):
        scaled_rows = scale_columns(upper_adj, layer_id)
        if layer_id % factor == 0:
            current = guess_wide[layer_id // factor] + spread[layer_id // factor].astype(
                jnp.float32
            )
        else:
            current = fine_step(upper_adj, scaled_rows, layer_id)
        adjoint_parts[layer_id] = lax.dynamic_slice_in_dim(current, col_start, columns, 1).astype(
            jnp.bfloat16
        )
        scaled_parts[layer_id] = scaled_rows
        upper_adj = current
    adjoint_out = jnp.stack(adjoint_parts)
    scaled_out = jnp.stack(scaled_parts)
    partial_terms = jnp.einsum(
        "lrd,lrh->ldh", states, scaled_out, preferred_element_type=jnp.float32
    )
    weight_grads = step_size * lax.psum_scatter(
        partial_terms.astype(jnp.bfloat16), "dp", scatter_dimension=1, tiled=True
    ).astype(jnp.float32)
    return (adjoint_out, weight_grads)


def solution(mesh):
    return jax.shard_map(
        body,
        mesh=mesh,
        in_specs=(
            P("layer", "dp", None),
            P("layer", "dp", "mp"),
            P("layer", "dp", None),
            P("dp", None),
        ),
        out_specs=(P("layer", "dp", "mp"), P("layer", "dp", "mp")),
        check_vma=False,
    )
```

profile of v0, /device:TPU:1, one launch (start us, length us, event | category | flops | bytes accessed | tf_op | source)
XLA Modules:
  0.0 934.7 jit_solution(8836864910243469288)
XLA Ops:
  8.0 8.7 collective-permute-start.1
  19.1 53.4 %all-gather.3.cloned.1.call-done = bf16[4,1024,512]{2,1,0:T(8,128)(2,1)} async-done(((bf16[4,128,512]{2,1,0:T(8,128)(2,1)}), bf16[4,1024,512]{2,1,0:T(8,128)(2,1)}) %all-gather.3.cloned.1.call-update) | async-done | bytes 4194320 | tf_op jit(solution)/shard_map/all_gather | solution.py:41
  78.4 59.1 %all-reduce.8.cloned.1.call-done = f32[128,1024]{1,0:T(8,128)} async-done(((f32[128,1024]{1,0:T(8,128)}), f32[128,1024]{1,0:T(8,128)}) %all-reduce.8.cloned.1.call-update) | async-done | bytes 524304 | tf_op jit(solution)/shard_map/psum | solution.py:54
  142.7 56.4 %all-reduce.10.cloned.1.call-done = f32[128,1024]{1,0:T(8,128)} async-done(((f32[128,1024]{1,0:T(8,128)}), f32[128,1024]{1,0:T(8,128)}) %all-reduce.10.cloned.1.call-update) | async-done | bytes 524304 | tf_op jit(solution)/shard_map/psum | solution.py:54
  207.4 53.4 %all-reduce.12.cloned.1.call-done = f32[128,1024]{1,0:T(8,128)} async-done(((f32[128,1024]{1,0:T(8,128)}), f32[128,1024]{1,0:T(8,128)}) %all-reduce.12.cloned.1.call-update) | async-done | bytes 524304 | tf_op jit(solution)/shard_map/psum | solution.py:54
  265.6 62.4 %all-gather.5.cloned.1.call-done = bf16[1,1024,1024]{2,1,0:T(8,128)(2,1)} async-done(((bf16[1,1024,512]{2,1,0:T(8,128)(2,1)}), bf16[1,1024,1024]{2,1,0:T(8,128)(2,1)}) %all-gather.5.cloned.1.call-update) | async-done | bytes 2097168 | tf_op jit(solution)/shard_map/all_gather | solution.py:67
  330.0 59.3 %all-reduce.14.cloned.1.call-done = f32[128,1024]{1,0:T(8,128)} async-done(((f32[128,1024]{1,0:T(8,128)}), f32[128,1024]{1,0:T(8,128)}) %all-reduce.14.cloned.1.call-update) | async-done | bytes 524304 | tf_op jit(solution)/shard_map/psum | solution.py:54
  390.3 250.6 %while.23 = (s32[]{:T(128)}, bf16[64,1024]{1,0:T(8,128)(2,1)S(1)}, bf16[1,64,1024]{2,1,0:T(8,128)(2,1)S(1)}, s32[]{:T(128)}, f32[64,1024]{1,0:T(8,128)S(1)}, /*i...) while((s32[]{:T(128)}, bf16[64,1024]{1,0:T(8,128)(2,1)S(1)}, ...), condition=%wide.region_7.8_spmd, body=%wide.region_4.7_spmd.sunk | while | flops 134742016 | bytes 3408051 | solution.py:99
  390.4 2.7 collective-permute-start
  393.1 3.9 collective-permute-done
  398.9 4.4 collective-permute-done
  405.2 4.4 collective-permute-done
  411.5 4.4 collective-permute-done
  417.7 4.4 collective-permute-done
  424.0 4.4 collective-permute-done
  430.3 4.4 collective-permute-done
  436.6 4.4 collective-permute-done
  442.8 4.4 collective-permute-done
  449.1 4.4 collective-permute-done
  455.4 4.4 collective-permute-done
  461.7 5.5 collective-permute-done
  469.0 6.5 collective-permute-done
  477.4 6.5 collective-permute-done
  485.8 6.5 collective-permute-done
  494.2 6.5 collective-permute-done
  502.6 6.5 collective-permute-done
  511.0 6.5 collective-permute-done
  519.4 6.5 collective-permute-done
  527.7 6.5 collective-permute-done
  536.1 6.5 collective-permute-done
  544.5 6.5 collective-permute-done
  552.9 6.5 collective-permute-done
  561.3 6.5 collective-permute-done
  569.7 6.5 collective-permute-done
  578.1 6.5 collective-permute-done
  586.5 6.5 collective-permute-done
  594.8 6.5 collective-permute-done
  603.2 6.5 collective-permute-done
  611.6 20.7 %collective-permute-done = bf16[64,1024]{1,0:T(8,128)(2,1)S(1)} collective-permute-done((bf16[64,1024]{1,0:T(8,128)(2,1)S(1)}, bf16[64,1024]{1,0:T(8,128)(2,1)S(1)}, u32[]{:S(2)}, u32[]{:S(2)}) %collective-permute-start) | collective-permute-done | bytes 131104 | tf_op jit(solution)/shard_map/while/body/eval_jaxpr/ppermute | solution.py:12
  636.6 4.4 collective-permute-done
  641.0 15.2 %all_gather.11 = bf16[2,128,1024]{2,1,0:T(8,128)(2,1)S(1)} all-gather(bf16[2,64,1024]{2,1,0:T(8,128)(2,1)S(1)} %pad_maximum_fusion.1), channel_id=1, replica_groups=mesh['layer'=32,'dp'=8,'mp'=2] {'mp'}, dimensions={1}, use_global_device_ids=true | all-gather | bytes 786432 | tf_op jit(solution)/shard_map/all_gather | solution.py:103
  658.9 69.1 %all-reduce.16.cloned.1.call-done = f32[128,1024]{1,0:T(8,128)} async-done(((f32[128,1024]{1,0:T(8,128)}), f32[128,1024]{1,0:T(8,128)}) %all-reduce.16.cloned.1.call-update) | async-done | bytes 524304 | tf_op jit(solution)/shard_map/psum | solution.py:54
  731.7 58.0 %all-reduce.18.cloned.1.call-done = f32[128,1024]{1,0:T(8,128)} async-done(((f32[128,1024]{1,0:T(8,128)}), f32[128,1024]{1,0:T(8,128)}) %all-reduce.18.cloned.1.call-update) | async-done | bytes 524304 | tf_op jit(solution)/shard_map/psum | solution.py:54
  793.4 58.0 %all-reduce.20.cloned.1.call-done = f32[128,1024]{1,0:T(8,128)} async-done(((f32[128,1024]{1,0:T(8,128)}), f32[128,1024]{1,0:T(8,128)}) %all-reduce.20.cloned.1.call-update) | async-done | bytes 524304 | tf_op jit(solution)/shard_map/psum | solution.py:54
  852.4 4.5 convert_bitcast_fusion
  856.9 7.8 copy.11
  864.7 5.6 copy.13
  871.3 53.3 %reduce-scatter.4.cloned.1.call-done = bf16[128,2048]{1,0:T(8,128)(2,1)} async-done(((bf16[1024,2048]{1,0:T(8,128)(2,1)}), bf16[128,2048]{1,0:T(8,128)(2,1)}) %reduce-scatter.4.cloned.1.call-update) | async-done | bytes 524304
  (132 shorter events, 107.6 us)
Async XLA Ops:
  7.2 69.6 %copy-start = (bf16[4,128,1024]{2,1,0:T(8,128)(2,1)S(1)}, bf16[4,128,1024]{2,1,0:T(8,128)(2,1)}, u32[]{:S(2)}) copy-start(bf16[4,128,1024]{2,1,0:T(8,128)(2,1)} %param.10) | copy-start | bytes 3145732
  7.2 65.3 %all-gather.3.cloned.1.call-start = ((), (), s32[]{:S(2)}) async-start(), calls=%async_computation.1 | async-start | bytes 4718592 | tf_op jit(solution)/shard_map/all_gather | solution.py:41
  7.9 129.6 %all-reduce.8.cloned.1.call-start = ((), (), s32[]{:S(2)}) async-start(), calls=%async_computation.3 | async-start | bytes 1048576 | tf_op jit(solution)/shard_map/psum | solution.py:54
  8.0 10.1 %collective-permute-start.1 = (bf16[128,1024]{1,0:T(8,128)(2,1)}, bf16[128,1024]{1,0:T(8,128)(2,1)S(1)}, u32[]{:S(2)}, u32[]{:S(2)}) collective-permute-start(bf16[128,1024]{1,0:T(8,128)(2,1)} %bitcast.126), channel_id=1, source_target_pairs={{16,0},{32,16},{48,32},{64,48},{80,64},{96,80},{112,96},{128,112},... | collective-permute-start | bytes 786440 | tf_op jit(solution)/shard_map/ppermute | solution.py:12
  74.1 4.2 copy-start.1
  76.8 122.4 %all-reduce.10.cloned.1.call-start = ((), (), s32[]{:S(2)}) async-start(), calls=%async_computation.4 | async-start | bytes 1048576 | tf_op jit(solution)/shard_map/psum | solution.py:54
  141.1 119.7 %all-reduce.12.cloned.1.call-start = ((), (), s32[]{:S(2)}) async-start(), calls=%async_computation.5 | async-start | bytes 1048576 | tf_op jit(solution)/shard_map/psum | solution.py:54
  202.8 125.2 %all-gather.5.cloned.1.call-start = ((), (), s32[]{:S(2)}) async-start(), calls=%async_computation.2 | async-start | bytes 3145728 | tf_op jit(solution)/shard_map/all_gather | solution.py:67
  205.1 122.9 %slice-start = ((bf16[4,128,1024]{2,1,0:T(8,128)(2,1)}), bf16[1,128,1024]{2,1,0:T(8,128)(2,1)S(1)}, s32[]{:S(2)}) async-start(bf16[4,128,1024]{2,1,0:T(8,128)(2,1)} %param.10), calls=%async_computation.11 | async-start | bytes 524288 | tf_op jit(solution)/shard_map/slice | solution.py:68
  205.1 184.2 %all-reduce.14.cloned.1.call-start = ((), (), s32[]{:S(2)}) async-start(), calls=%async_computation.6 | async-start | bytes 1048576 | tf_op jit(solution)/shard_map/psum | solution.py:54
  264.5 463.5 %all-reduce.16.cloned.1.call-start = ((), (), s32[]{:S(2)}) async-start(), calls=%async_computation.7 | async-start | bytes 1048576 | tf_op jit(solution)/shard_map/psum | solution.py:54
  390.4 6.6 collective-permute-start
  397.0 6.3 collective-permute-start
  403.3 6.3 collective-permute-start
  409.5 6.3 collective-permute-start
  415.8 6.3 collective-permute-start
  422.1 6.3 collective-permute-start
  428.4 6.3 collective-permute-start
  434.6 6.3 collective-permute-start
  440.9 6.3 collective-permute-start
  447.2 6.3 collective-permute-start
  453.5 6.3 collective-permute-start
  459.8 7.4 collective-permute-start
  467.1 8.4 collective-permute-start
  475.5 8.4 collective-permute-start
  483.9 8.4 collective-permute-start
  492.3 8.4 collective-permute-start
  500.7 8.4 collective-permute-start
  509.1 8.4 collective-permute-start
  517.4 8.4 collective-permute-start
  525.8 8.4 collective-permute-start
  534.2 8.4 collective-permute-start
  542.6 8.4 collective-permute-start
  551.0 8.4 collective-permute-start
  559.4 8.4 collective-permute-start
  567.8 8.4 collective-permute-start
  576.1 8.4 collective-permute-start
  584.5 8.4 collective-permute-start
  592.9 8.4 collective-permute-start
  601.3 8.4 collective-permute-start
  609.7 22.6 %collective-permute-start = (bf16[64,1024]{1,0:T(8,128)(2,1)S(1)}, bf16[64,1024]{1,0:T(8,128)(2,1)S(1)}, u32[]{:S(2)}, u32[]{:S(2)}) collective-permute-start(bf16[64,1024]{1,0:T(8,128)(2,1)S(1)} %bitcast.125), channel_id=1, source_target_pairs={{16,0},{32,16},{48,32},{64,48},{80,64},{96,80},{112,96},{128,112},... | collective-permute-start | bytes 393224 | tf_op jit(solution)/shard_map/while/body/eval_jaxpr/ppermute | solution.py:12
  634.6 6.3 collective-permute-start
  640.9 15.3 %copy-start.2 = (f32[128,512]{1,0:T(8,128)S(1)}, f32[128,512]{1,0:T(8,128)}, u32[]{:S(2)}) copy-start(f32[128,512]{1,0:T(8,128)} %copy-done.1) | copy-start | bytes 786436
  658.8 192.6 %copy-start.3 = (f32[128,512]{1,0:T(8,128)S(1)}, f32[128,512]{1,0:T(8,128)}, u32[]{:S(2)}) copy-start(f32[128,512]{1,0:T(8,128)} %fusion.56) | copy-start | bytes 786436
  658.9 130.8 %all-reduce.18.cloned.1.call-start = ((), (), s32[]{:S(2)}) async-start(), calls=%async_computation.8 | async-start | bytes 1048576 | tf_op jit(solution)/shard_map/psum | solution.py:54
  731.7 119.7 %all-reduce.20.cloned.1.call-start = ((), (), s32[]{:S(2)}) async-start(), calls=%async_computation.9 | async-start | bytes 1048576 | tf_op jit(solution)/shard_map/psum | solution.py:54
  793.4 131.2 %reduce-scatter.4.cloned.1.call-start = ((), (), s32[]{:S(2)}) async-start(), calls=%async_computation.10 | async-start | bytes 4718592
Sparse Core Ops, SparseCore 0:
  10.1 62.3 all-gather.2
  76.9 60.5 all-reduce.7
  141.2 57.8 all-reduce.9
  202.9 57.8 all-reduce.11
  263.3 64.5 all-gather.4
  331.3 57.9 all-reduce.13
  659.0 68.9 all-reduce.15
  731.8 57.8 all-reduce.17
  793.5 57.8 all-reduce.19
  870.4 54.0 reduce-scatter.3
where the time goes:
time: 937 us; the launch traced here: 935 us
  waiting for transfers between devices  772 us (82%)
  starting transfers between devices  69.2 us (7%)
  matrix products  33.6 us (4%)
  local copies, waits for them, and re-layouts  18.9 us (2%)
  blocking collectives  15.2 us (2%)
  between operations  14.4 us (2%)
  other arithmetic  10.7 us (1%)
    psum x7, waiting for transfers between devices, fine_step(): summed = lax.psum(back_product(scaled_rows, gathered[layer_id]), 'mp')  413 us
    ppermute x32, waiting for transfers between devices, from_behind(): lax.ppermute(value, axis, [(source, source + steps) for source in range(l...  189 us
    ppermute x32, starting transfers between devices, from_behind(): lax.ppermute(value, axis, [(source, source + steps) for source in range(l...  68.8 us
    all_gather x1, waiting for transfers between devices, body(): lax.all_gather(gathered[::factor], 'mp', axis=2, tiled=True)  62.4 us
    unnamed x11, waiting for transfers between devices  54.1 us
    all_gather x1, waiting for transfers between devices, body(): gathered = lax.all_gather(weights, 'dp', axis=1, tiled=True)  53.4 us
    dot_general x8, matrix products, back_product(): lax.dot_general(scaled_rows, weight_block, (((1,), (1,)), ((), ())), pref...  20 us
  transfers between devices with their start and end apart: 42, of which 42 were waited for; matrix products, arithmetic and copies ran while one was open for 2% of the time, Pallas kernels for 0%

commit v1 on v0

--- a/solution.py
+++ b/solution.py
@@ -51,7 +51,9 @@
         return (own_part * slopes[layer_id]).astype(jnp.bfloat16)
 
     def fine_step(upper_adj, scaled_rows, layer_id):
-        summed = lax.psum(back_product(scaled_rows, gathered[layer_id]), "mp")
+        summed = jnp.sum(
+            lax.all_gather(back_product(scaled_rows, gathered[layer_id]), "mp"), axis=0
+        )
         return upper_adj + step_size * summed
 
     upper_adj = terminal

time: 937 us -> 833 us (0.89)
  waiting for transfers between devices: 772 us -> 663 us
    psum x7 -> x0, waiting for transfers between devices: 413 us -> none  [fine_step(): summed = lax.psum(back_product(scaled_rows, gathered[layer_id]), 'mp')]
    all_gather x0 -> x7, waiting for transfers between devices: none -> 306 us  [fine_step(): lax.all_gather(back_product(scaled_rows, gathered[layer_id]), 'mp')]
    reduce_sum x0 -> x7, other arithmetic: none -> 10.3 us  [fine_step(): jnp.sum(lax.all_gather(back_product(scaled_rows, gathered[layer_id]), 'mp...]
where the time goes in v1:
time: 833 us; the launch traced here: 831 us
  waiting for transfers between devices  663 us (80%)
  starting transfers between devices  69.2 us (8%)
  matrix products  31.8 us (4%)
  local copies, waits for them, and re-layouts  21.3 us (3%)
  other arithmetic  19.3 us (2%)
  between operations  14.5 us (2%)
  blocking collectives  11.6 us (1%)
    all_gather x7, waiting for transfers between devices, fine_step(): lax.all_gather(back_product(scaled_rows, gathered[layer_id]), 'mp')  306 us
    ppermute x32, waiting for transfers between devices, from_behind(): lax.ppermute(value, axis, [(source, source + steps) for source in range(l...  190 us
    ppermute x32, starting transfers between devices, from_behind(): lax.ppermute(value, axis, [(source, source + steps) for source in range(l...  68.8 us
    all_gather x1, waiting for transfers between devices, body(): lax.all_gather(gathered[::factor], 'mp', axis=2, tiled=True)  60.9 us
    all_gather x1, waiting for transfers between devices, body(): gathered = lax.all_gather(weights, 'dp', axis=1, tiled=True)  53.4 us
    unnamed x11, waiting for transfers between devices  53 us
    dot_general x8, matrix products, back_product(): lax.dot_general(scaled_rows, weight_block, (((1,), (1,)), ((), ())), pref...  19.2 us
    unnamed x28, local copies, waits for them, and re-layouts  18.3 us
  transfers between devices with their start and end apart: 42, of which 42 were waited for; matrix products, arithmetic and copies ran while one was open for 2% of the time, Pallas kernels for 0%

profile of v1, /device:TPU:1, one launch (start us, length us, event | category | flops | bytes accessed | tf_op | source)
XLA Modules:
  0.0 830.8 jit_solution(10649964009465406608)
XLA Ops:
  8.0 8.7 %collective-permute-start.1 = (bf16[128,1024]{1,0:T(8,128)(2,1)}, bf16[128,1024]{1,0:T(8,128)(2,1)S(1)}, u32[]{:S(2)}, u32[]{:S(2)}) collective-permute-start(bf16[128,1024]{1,0:T(8,128)(2,1)} %bitcast.139), channel_id=1, source_target_pairs={{16,0},{32,16},{48,32},{64,48},{80,64},{96,80},{112,96},{128,112},... | collective-permute-start | bytes 786440 | tf_op jit(solution)/shard_map/ppermute | solution.py:12
  19.1 53.4 %all-gather.17.cloned.1.call-done = bf16[4,1024,512]{2,1,0:T(8,128)(2,1)} async-done(((bf16[4,128,512]{2,1,0:T(8,128)(2,1)}), bf16[4,1024,512]{2,1,0:T(8,128)(2,1)}) %all-gather.17.cloned.1.call-update) | async-done | bytes 4194320 | tf_op jit(solution)/shard_map/all_gather | solution.py:41
  79.0 42.6 %all-gather.21.cloned.1.call-done = f32[256,1024]{1,0:T(8,128)} async-done(((f32[128,1024]{1,0:T(8,128)}), f32[256,1024]{1,0:T(8,128)}) %all-gather.21.cloned.1.call-update) | async-done | bytes 1048592 | tf_op jit(solution)/shard_map/all_gather | solution.py:55
  127.2 39.9 %all-gather.23.cloned.1.call-done = f32[256,1024]{1,0:T(8,128)} async-done(((f32[128,1024]{1,0:T(8,128)}), f32[256,1024]{1,0:T(8,128)}) %all-gather.23.cloned.1.call-update) | async-done | bytes 1048592 | tf_op jit(solution)/shard_map/all_gather | solution.py:55
  175.7 36.8 %all-gather.25.cloned.1.call-done = f32[256,1024]{1,0:T(8,128)} async-done(((f32[128,1024]{1,0:T(8,128)}), f32[256,1024]{1,0:T(8,128)}) %all-gather.25.cloned.1.call-update) | async-done | bytes 1048592 | tf_op jit(solution)/shard_map/all_gather | solution.py:55
  213.9 2.8 fusion.57
  218.6 60.9 %all-gather.19.cloned.1.call-done = bf16[1,1024,1024]{2,1,0:T(8,128)(2,1)} async-done(((bf16[1,1024,512]{2,1,0:T(8,128)(2,1)}), bf16[1,1024,1024]{2,1,0:T(8,128)(2,1)}) %all-gather.19.cloned.1.call-update) | async-done | bytes 2097168 | tf_op jit(solution)/shard_map/all_gather | solution.py:69
  281.7 41.3 %all-gather.27.cloned.1.call-done = f32[256,1024]{1,0:T(8,128)} async-done(((f32[128,1024]{1,0:T(8,128)}), f32[256,1024]{1,0:T(8,128)}) %all-gather.27.cloned.1.call-update) | async-done | bytes 1048592 | tf_op jit(solution)/shard_map/all_gather | solution.py:55
  327.0 250.4 %while.23 = (s32[]{:T(128)}, bf16[64,1024]{1,0:T(8,128)(2,1)S(1)}, bf16[1,64,1024]{2,1,0:T(8,128)(2,1)}, s32[]{:T(128)}, f32[64,1024]{1,0:T(8,128)S(1)}, /*index...) while((s32[]{:T(128)}, bf16[64,1024]{1,0:T(8,128)(2,1)S(1)}, ...), condition=%wide.region_7.8_spmd, body=%wide.region_4.7_spmd.sunk | while | flops 134742016 | bytes 3408051 | solution.py:101
  329.8 3.9 collective-permute-done
  335.6 4.6 collective-permute-done
  342.1 4.6 collective-permute-done
  348.6 4.6 collective-permute-done
  355.1 4.6 collective-permute-done
  361.6 4.6 collective-permute-done
  368.1 4.6 collective-permute-done
  374.6 4.6 collective-permute-done
  381.0 4.6 collective-permute-done
  387.5 4.6 collective-permute-done
  394.0 4.6 collective-permute-done
  400.5 5.7 collective-permute-done
  408.1 6.7 collective-permute-done
  416.7 6.7 collective-permute-done
  425.3 6.7 collective-permute-done
  433.9 6.7 collective-permute-done
  442.5 6.7 collective-permute-done
  451.1 6.7 collective-permute-done
  459.7 6.7 collective-permute-done
  468.3 6.7 collective-permute-done
  476.9 6.7 collective-permute-done
  485.5 6.7 collective-permute-done
  494.1 6.7 collective-permute-done
  502.6 6.7 collective-permute-done
  511.2 6.7 collective-permute-done
  519.8 6.7 collective-permute-done
  528.4 6.7 collective-permute-done
  537.0 6.7 collective-permute-done
  545.6 6.7 collective-permute-done
  554.2 15.2 %collective-permute-done = bf16[64,1024]{1,0:T(8,128)(2,1)S(1)} collective-permute-done((bf16[64,1024]{1,0:T(8,128)(2,1)}, bf16[64,1024]{1,0:T(8,128)(2,1)S(1)}, u32[]{:S(2)}, u32[]{:S(2)}) %collective-permute-start) | collective-permute-done | bytes 131104 | tf_op jit(solution)/shard_map/while/body/eval_jaxpr/ppermute | solution.py:12
  572.8 4.6 collective-permute-done
  578.4 11.6 %all_gather.61 = bf16[2,128,1024]{2,1,0:T(8,128)(2,1)S(1)} all-gather(bf16[2,64,1024]{2,1,0:T(8,128)(2,1)S(1)} %pad_maximum_fusion.1), channel_id=1, replica_groups=mesh['layer'=32,'dp'=8,'mp'=2] {'mp'}, dimensions={1}, use_global_device_ids=true | all-gather | bytes 786432 | tf_op jit(solution)/shard_map/all_gather | solution.py:105
  592.6 62.2 %all-gather.29.cloned.1.call-done = f32[256,1024]{1,0:T(8,128)} async-done(((f32[128,1024]{1,0:T(8,128)}), f32[256,1024]{1,0:T(8,128)}) %all-gather.29.cloned.1.call-update) | async-done | bytes 1048592 | tf_op jit(solution)/shard_map/all_gather | solution.py:55
  658.8 41.4 %all-gather.31.cloned.1.call-done = f32[256,1024]{1,0:T(8,128)} async-done(((f32[128,1024]{1,0:T(8,128)}), f32[256,1024]{1,0:T(8,128)}) %all-gather.31.cloned.1.call-update) | async-done | bytes 1048592 | tf_op jit(solution)/shard_map/all_gather | solution.py:55
  705.3 41.4 %all-gather.33.cloned.1.call-done = f32[256,1024]{1,0:T(8,128)} async-done(((f32[128,1024]{1,0:T(8,128)}), f32[256,1024]{1,0:T(8,128)}) %all-gather.33.cloned.1.call-update) | async-done | bytes 1048592 | tf_op jit(solution)/shard_map/all_gather | solution.py:55
  749.8 3.3 convert_bitcast_fusion
  753.1 7.8 copy.11
  760.9 5.6 copy.13
  768.6 52.1 %reduce-scatter.4.cloned.1.call-done = bf16[128,2048]{1,0:T(8,128)(2,1)} async-done(((bf16[1024,2048]{1,0:T(8,128)(2,1)}), bf16[128,2048]{1,0:T(8,128)(2,1)}) %reduce-scatter.4.cloned.1.call-update) | async-done | bytes 524304
  (153 shorter events, 116.9 us)
Async XLA Ops:
  7.2 70.2 %copy-start.3 = (bf16[4,128,1024]{2,1,0:T(8,128)(2,1)S(1)}, bf16[4,128,1024]{2,1,0:T(8,128)(2,1)}, u32[]{:S(2)}) copy-start(bf16[4,128,1024]{2,1,0:T(8,128)(2,1)} %param.10) | copy-start | bytes 3145732
  7.2 65.3 %all-gather.17.cloned.1.call-start = ((), (), s32[]{:S(2)}) async-start(), calls=%async_computation.1 | async-start | bytes 4718592 | tf_op jit(solution)/shard_map/all_gather | solution.py:41
  7.9 113.7 %all-gather.21.cloned.1.call-start = ((), (), s32[]{:S(2)}) async-start(), calls=%async_computation.3 | async-start | bytes 1572864 | tf_op jit(solution)/shard_map/all_gather | solution.py:55
  8.0 10.1 %collective-permute-start.1 = (bf16[128,1024]{1,0:T(8,128)(2,1)}, bf16[128,1024]{1,0:T(8,128)(2,1)S(1)}, u32[]{:S(2)}, u32[]{:S(2)}) collective-permute-start(bf16[128,1024]{1,0:T(8,128)(2,1)} %bitcast.139), channel_id=1, source_target_pairs={{16,0},{32,16},{48,32},{64,48},{80,64},{96,80},{112,96},{128,112},... | collective-permute-start | bytes 786440 | tf_op jit(solution)/shard_map/ppermute | solution.py:12
  77.3 89.7 %all-gather.23.cloned.1.call-start = ((), (), s32[]{:S(2)}) async-start(), calls=%async_computation.4 | async-start | bytes 1572864 | tf_op jit(solution)/shard_map/all_gather | solution.py:55
  79.0 88.1 %copy-start.6 = (f32[128,512]{1,0:T(8,128)}, f32[128,512]{1,0:T(8,128)S(1)}, u32[]{:S(2)}) copy-start(f32[128,512]{1,0:T(8,128)S(1)} %fusion.54) | copy-start | bytes 786436
  125.5 86.9 %all-gather.25.cloned.1.call-start = ((), (), s32[]{:S(2)}) async-start(), calls=%async_computation.5 | async-start | bytes 1572864 | tf_op jit(solution)/shard_map/all_gather | solution.py:55
  171.0 108.5 %all-gather.19.cloned.1.call-start = ((), (), s32[]{:S(2)}) async-start(), calls=%async_computation.2 | async-start | bytes 3145728 | tf_op jit(solution)/shard_map/all_gather | solution.py:69
  173.3 106.2 %slice-start = ((bf16[4,128,1024]{2,1,0:T(8,128)(2,1)}), bf16[1,128,1024]{2,1,0:T(8,128)(2,1)S(1)}, s32[]{:S(2)}) async-start(bf16[4,128,1024]{2,1,0:T(8,128)(2,1)} %param.10), calls=%async_computation.11 | async-start | bytes 524288 | tf_op jit(solution)/shard_map/slice | solution.py:70
  173.3 149.7 %all-gather.27.cloned.1.call-start = ((), (), s32[]{:S(2)}) async-start(), calls=%async_computation.6 | async-start | bytes 1572864 | tf_op jit(solution)/shard_map/all_gather | solution.py:55
  216.7 438.0 %all-gather.29.cloned.1.call-start = ((), (), s32[]{:S(2)}) async-start(), calls=%async_computation.7 | async-start | bytes 1572864 | tf_op jit(solution)/shard_map/all_gather | solution.py:55
  279.5 47.5 %copy-start = (bf16[1,1024,1024]{2,1,0:T(8,128)(2,1)S(1)}, bf16[1,1024,1024]{2,1,0:T(8,128)(2,1)}, u32[]{:S(2)}) copy-start(bf16[1,1024,1024]{2,1,0:T(8,128)(2,1)} %all-gather.19.cloned.1.call-done) | copy-start | bytes 6291460
  327.0 6.7 collective-permute-start
  333.7 6.5 collective-permute-start
  340.2 6.5 collective-permute-start
  346.7 6.5 collective-permute-start
  353.2 6.5 collective-permute-start
  359.7 6.5 collective-permute-start
  366.2 6.5 collective-permute-start
  372.6 6.5 collective-permute-start
  379.1 6.5 collective-permute-start
  385.6 6.5 collective-permute-start
  392.1 6.5 collective-permute-start
  398.6 7.6 collective-permute-start
  406.2 8.6 %collective-permute-start = (bf16[64,1024]{1,0:T(8,128)(2,1)}, bf16[64,1024]{1,0:T(8,128)(2,1)S(1)}, u32[]{:S(2)}, u32[]{:S(2)}) collective-permute-start(bf16[64,1024]{1,0:T(8,128)(2,1)} %bitcast.124), channel_id=1, source_target_pairs={{16,0},{32,16},{48,32},{64,48},{80,64},{96,80},{112,96},{128,112},... | collective-permute-start | bytes 393224 | tf_op jit(solution)/shard_map/while/body/eval_jaxpr/ppermute | solution.py:12
  414.8 8.6 %collective-permute-start = (bf16[64,1024]{1,0:T(8,128)(2,1)}, bf16[64,1024]{1,0:T(8,128)(2,1)S(1)}, u32[]{:S(2)}, u32[]{:S(2)}) collective-permute-start(bf16[64,1024]{1,0:T(8,128)(2,1)} %bitcast.124), channel_id=1, source_target_pairs={{16,0},{32,16},{48,32},{64,48},{80,64},{96,80},{112,96},{128,112},... | collective-permute-start | bytes 393224 | tf_op jit(solution)/shard_map/while/body/eval_jaxpr/ppermute | solution.py:12
  423.4 8.6 %collective-permute-start = (bf16[64,1024]{1,0:T(8,128)(2,1)}, bf16[64,1024]{1,0:T(8,128)(2,1)S(1)}, u32[]{:S(2)}, u32[]{:S(2)}) collective-permute-start(bf16[64,1024]{1,0:T(8,128)(2,1)} %bitcast.124), channel_id=1, source_target_pairs={{16,0},{32,16},{48,32},{64,48},{80,64},{96,80},{112,96},{128,112},... | collective-permute-start | bytes 393224 | tf_op jit(solution)/shard_map/while/body/eval_jaxpr/ppermute | solution.py:12
  432.0 8.6 %collective-permute-start = (bf16[64,1024]{1,0:T(8,128)(2,1)}, bf16[64,1024]{1,0:T(8,128)(2,1)S(1)}, u32[]{:S(2)}, u32[]{:S(2)}) collective-permute-start(bf16[64,1024]{1,0:T(8,128)(2,1)} %bitcast.124), channel_id=1, source_target_pairs={{16,0},{32,16},{48,32},{64,48},{80,64},{96,80},{112,96},{128,112},... | collective-permute-start | bytes 393224 | tf_op jit(solution)/shard_map/while/body/eval_jaxpr/ppermute | solution.py:12
  440.6 8.6 %collective-permute-start = (bf16[64,1024]{1,0:T(8,128)(2,1)}, bf16[64,1024]{1,0:T(8,128)(2,1)S(1)}, u32[]{:S(2)}, u32[]{:S(2)}) collective-permute-start(bf16[64,1024]{1,0:T(8,128)(2,1)} %bitcast.124), channel_id=1, source_target_pairs={{16,0},{32,16},{48,32},{64,48},{80,64},{96,80},{112,96},{128,112},... | collective-permute-start | bytes 393224 | tf_op jit(solution)/shard_map/while/body/eval_jaxpr/ppermute | solution.py:12
  449.2 8.6 %collective-permute-start = (bf16[64,1024]{1,0:T(8,128)(2,1)}, bf16[64,1024]{1,0:T(8,128)(2,1)S(1)}, u32[]{:S(2)}, u32[]{:S(2)}) collective-permute-start(bf16[64,1024]{1,0:T(8,128)(2,1)} %bitcast.124), channel_id=1, source_target_pairs={{16,0},{32,16},{48,32},{64,48},{80,64},{96,80},{112,96},{128,112},... | collective-permute-start | bytes 393224 | tf_op jit(solution)/shard_map/while/body/eval_jaxpr/ppermute | solution.py:12
  457.7 8.6 %collective-permute-start = (bf16[64,1024]{1,0:T(8,128)(2,1)}, bf16[64,1024]{1,0:T(8,128)(2,1)S(1)}, u32[]{:S(2)}, u32[]{:S(2)}) collective-permute-start(bf16[64,1024]{1,0:T(8,128)(2,1)} %bitcast.124), channel_id=1, source_target_pairs={{16,0},{32,16},{48,32},{64,48},{80,64},{96,80},{112,96},{128,112},... | collective-permute-start | bytes 393224 | tf_op jit(solution)/shard_map/while/body/eval_jaxpr/ppermute | solution.py:12
  466.3 8.6 %collective-permute-start = (bf16[64,1024]{1,0:T(8,128)(2,1)}, bf16[64,1024]{1,0:T(8,128)(2,1)S(1)}, u32[]{:S(2)}, u32[]{:S(2)}) collective-permute-start(bf16[64,1024]{1,0:T(8,128)(2,1)} %bitcast.124), channel_id=1, source_target_pairs={{16,0},{32,16},{48,32},{64,48},{80,64},{96,80},{112,96},{128,112},... | collective-permute-start | bytes 393224 | tf_op jit(solution)/shard_map/while/body/eval_jaxpr/ppermute | solution.py:12
  474.9 8.6 %collective-permute-start = (bf16[64,1024]{1,0:T(8,128)(2,1)}, bf16[64,1024]{1,0:T(8,128)(2,1)S(1)}, u32[]{:S(2)}, u32[]{:S(2)}) collective-permute-start(bf16[64,1024]{1,0:T(8,128)(2,1)} %bitcast.124), channel_id=1, source_target_pairs={{16,0},{32,16},{48,32},{64,48},{80,64},{96,80},{112,96},{128,112},... | collective-permute-start | bytes 393224 | tf_op jit(solution)/shard_map/while/body/eval_jaxpr/ppermute | solution.py:12
  483.5 8.6 %collective-permute-start = (bf16[64,1024]{1,0:T(8,128)(2,1)}, bf16[64,1024]{1,0:T(8,128)(2,1)S(1)}, u32[]{:S(2)}, u32[]{:S(2)}) collective-permute-start(bf16[64,1024]{1,0:T(8,128)(2,1)} %bitcast.124), channel_id=1, source_target_pairs={{16,0},{32,16},{48,32},{64,48},{80,64},{96,80},{112,96},{128,112},... | collective-permute-start | bytes 393224 | tf_op jit(solution)/shard_map/while/body/eval_jaxpr/ppermute | solution.py:12
  492.1 8.6 %collective-permute-start = (bf16[64,1024]{1,0:T(8,128)(2,1)}, bf16[64,1024]{1,0:T(8,128)(2,1)S(1)}, u32[]{:S(2)}, u32[]{:S(2)}) collective-permute-start(bf16[64,1024]{1,0:T(8,128)(2,1)} %bitcast.124), channel_id=1, source_target_pairs={{16,0},{32,16},{48,32},{64,48},{80,64},{96,80},{112,96},{128,112},... | collective-permute-start | bytes 393224 | tf_op jit(solution)/shard_map/while/body/eval_jaxpr/ppermute | solution.py:12
  500.7 8.6 %collective-permute-start = (bf16[64,1024]{1,0:T(8,128)(2,1)}, bf16[64,1024]{1,0:T(8,128)(2,1)S(1)}, u32[]{:S(2)}, u32[]{:S(2)}) collective-permute-start(bf16[64,1024]{1,0:T(8,128)(2,1)} %bitcast.124), channel_id=1, source_target_pairs={{16,0},{32,16},{48,32},{64,48},{80,64},{96,80},{112,96},{128,112},... | collective-permute-start | bytes 393224 | tf_op jit(solution)/shard_map/while/body/eval_jaxpr/ppermute | solution.py:12
  509.3 8.6 %collective-permute-start = (bf16[64,1024]{1,0:T(8,128)(2,1)}, bf16[64,1024]{1,0:T(8,128)(2,1)S(1)}, u32[]{:S(2)}, u32[]{:S(2)}) collective-permute-start(bf16[64,1024]{1,0:T(8,128)(2,1)} %bitcast.124), channel_id=1, source_target_pairs={{16,0},{32,16},{48,32},{64,48},{80,64},{96,80},{112,96},{128,112},... | collective-permute-start | bytes 393224 | tf_op jit(solution)/shard_map/while/body/eval_jaxpr/ppermute | solution.py:12
  517.9 8.6 %collective-permute-start = (bf16[64,1024]{1,0:T(8,128)(2,1)}, bf16[64,1024]{1,0:T(8,128)(2,1)S(1)}, u32[]{:S(2)}, u32[]{:S(2)}) collective-permute-start(bf16[64,1024]{1,0:T(8,128)(2,1)} %bitcast.124), channel_id=1, source_target_pairs={{16,0},{32,16},{48,32},{64,48},{80,64},{96,80},{112,96},{128,112},... | collective-permute-start | bytes 393224 | tf_op jit(solution)/shard_map/while/body/eval_jaxpr/ppermute | solution.py:12
  526.5 8.6 %collective-permute-start = (bf16[64,1024]{1,0:T(8,128)(2,1)}, bf16[64,1024]{1,0:T(8,128)(2,1)S(1)}, u32[]{:S(2)}, u32[]{:S(2)}) collective-permute-start(bf16[64,1024]{1,0:T(8,128)(2,1)} %bitcast.124), channel_id=1, source_target_pairs={{16,0},{32,16},{48,32},{64,48},{80,64},{96,80},{112,96},{128,112},... | collective-permute-start | bytes 393224 | tf_op jit(solution)/shard_map/while/body/eval_jaxpr/ppermute | solution.py:12
  535.1 8.6 %collective-permute-start = (bf16[64,1024]{1,0:T(8,128)(2,1)}, bf16[64,1024]{1,0:T(8,128)(2,1)S(1)}, u32[]{:S(2)}, u32[]{:S(2)}) collective-permute-start(bf16[64,1024]{1,0:T(8,128)(2,1)} %bitcast.124), channel_id=1, source_target_pairs={{16,0},{32,16},{48,32},{64,48},{80,64},{96,80},{112,96},{128,112},... | collective-permute-start | bytes 393224 | tf_op jit(solution)/shard_map/while/body/eval_jaxpr/ppermute | solution.py:12
  543.7 8.6 %collective-permute-start = (bf16[64,1024]{1,0:T(8,128)(2,1)}, bf16[64,1024]{1,0:T(8,128)(2,1)S(1)}, u32[]{:S(2)}, u32[]{:S(2)}) collective-permute-start(bf16[64,1024]{1,0:T(8,128)(2,1)} %bitcast.124), channel_id=1, source_target_pairs={{16,0},{32,16},{48,32},{64,48},{80,64},{96,80},{112,96},{128,112},... | collective-permute-start | bytes 393224 | tf_op jit(solution)/shard_map/while/body/eval_jaxpr/ppermute | solution.py:12
  552.3 17.1 %collective-permute-start = (bf16[64,1024]{1,0:T(8,128)(2,1)}, bf16[64,1024]{1,0:T(8,128)(2,1)S(1)}, u32[]{:S(2)}, u32[]{:S(2)}) collective-permute-start(bf16[64,1024]{1,0:T(8,128)(2,1)} %bitcast.124), channel_id=1, source_target_pairs={{16,0},{32,16},{48,32},{64,48},{80,64},{96,80},{112,96},{128,112},... | collective-permute-start | bytes 393224 | tf_op jit(solution)/shard_map/while/body/eval_jaxpr/ppermute | solution.py:12
  570.9 6.5 collective-permute-start
  578.3 77.8 %copy-start.7 = (f32[128,512]{1,0:T(8,128)S(1)}, f32[128,512]{1,0:T(8,128)}, u32[]{:S(2)}) copy-start(f32[128,512]{1,0:T(8,128)} %copy-done.6) | copy-start | bytes 786436
  592.5 107.7 %all-gather.31.cloned.1.call-start = ((), (), s32[]{:S(2)}) async-start(), calls=%async_computation.8 | async-start | bytes 1572864 | tf_op jit(solution)/shard_map/all_gather | solution.py:55
  658.8 88.0 %all-gather.33.cloned.1.call-start = ((), (), s32[]{:S(2)}) async-start(), calls=%async_computation.9 | async-start | bytes 1572864 | tf_op jit(solution)/shard_map/all_gather | solution.py:55
  700.2 49.5 %copy-start.4 = (bf16[4,128,1024]{2,1,0:T(8,128)(2,1)S(1)}, bf16[4,128,1024]{2,1,0:T(8,128)(2,1)}, u32[]{:S(2)}) copy-start(bf16[4,128,1024]{2,1,0:T(8,128)(2,1)} %param.10) | copy-start | bytes 3145732
  705.3 115.4 %reduce-scatter.4.cloned.1.call-start = ((), (), s32[]{:S(2)}) async-start(), calls=%async_computation.10 | async-start | bytes 4718592
  (6 other events, 66.4 us)
Sparse Core Ops, SparseCore 0:
  10.1 62.3 all-gather.16
  77.5 44.0 all-gather.20
  125.7 41.3 all-gather.22
  171.1 41.2 all-gather.24
  215.0 64.4 all-gather.18
  281.4 41.5 all-gather.26
  592.7 62.0 all-gather.28
  658.9 41.3 all-gather.30
  705.4 41.2 all-gather.32
  766.7 53.9 reduce-scatter.3
